TPU v7x, 128 devices: a whole 4x4x4 slice. The times are simulated.
128 devices in a mesh: row: 8 (over x, core), col: 16 (over y, z).
Axes of the slice: x: 4, y: 4, z: 4, core: 2. Of those that a mesh axis runs over, the one named last changes fastest.
Arguments:
- right_side: float32 [131072, 128], P(('row', 'col')), may hold values from -6 to 6
- leaf_inverse: bfloat16 [131072, 1024], P(('row', 'col')), may hold values from -0.1875 to 0.1875
- compress: bfloat16 [131072, 2048], P(('row', 'col')), may hold values from -0.1875 to 0.1875
- middle: bfloat16 [262144, 2048], P(('row', 'col')), may hold values from -0.125 to 0.125
- expand: bfloat16 [131072, 2048], P(('row', 'col')), may hold values from -0.125 to 0.125
- row_project: bfloat16 [3, 131072, 256], P(None, ('row', 'col')), may hold values from -0.1875 to 0.1875
- row_expand: bfloat16 [3, 131072, 256], P(None, ('row', 'col')), may hold values from -0.25 to 0.25
- root_project: bfloat16 [131072, 256], P(('row', 'col')), may hold values from -0.015625 to 0.015625
- root_expand: bfloat16 [131072, 256], P(('row', 'col')), may hold values from -0.375 to 0.375
- owner_map: int32 [16], replicated, may hold values from 0 to 15, each once
Outputs:
- applied: float32 [131072, 128], P(('row', 'col'))
Inputs may be any that keep to these rules, and one draw needn't show every extreme that they name: owner_map names each of the 16 column positions exactly once.
All inputs are finite; a program needn't handle non-finite values.
Results may differ from a plain program's by a relative error of at most 0.004.
Values may be sent and summed in bfloat16 or wider, within the bound.
A program may use at most 128 MiB of HBM per device.

v0:
```python
import jax
import jax.numpy as jnp
from jax import lax
from jax.sharding import PartitionSpec as P

contract_first = (((0,), (0,)), ((), ()))


def swapped(x, axis, bit):
    return lax.ppermute(x, axis, [(i, i ^ 1 << bit) for i in range(lax.axis_size(axis))])


def per_device(
    right_side,
    leaf_inverse,
    compress,
    middle,
    expand,
    row_project,
    row_expand,
    root_project,
    root_expand,
    owner_map,
):
    lowered = right_side.astype(jnp.bfloat16)
    columns = lowered.shape[1]
    dense_part = jnp.dot(leaf_inverse, lowered, preferred_element_type=jnp.float32)
    coeffs = lax.dot_general(
        compress, lowered, contract_first, preferred_element_type=jnp.float32
    ).astype(jnp.bfloat16)
    col_count = lax.axis_size("col")
    pieces = coeffs.reshape(col_count, -1, columns)
    inverse = jnp.argsort(owner_map)
    outgoing = jnp.take(pieces, inverse, axis=0)
    arrived = lax.all_to_all(outgoing, "col", split_axis=0, concat_axis=0, tiled=True)
    shape_now = arrived.shape
    mixed_rows = jnp.dot(
        middle, arrived.reshape(-1, shape_now[2]), preferred_element_type=jnp.float32
    )
    mixed_rows = mixed_rows.astype(jnp.bfloat16).reshape(shape_now)
    returned = lax.all_to_all(mixed_rows, "col", split_axis=0, concat_axis=0, tiled=True)
    ordered = jnp.take(returned, owner_map, axis=0).reshape(-1, columns)
    cluster_part = jnp.dot(expand, ordered, preferred_element_type=jnp.float32)
    level_coeffs = jnp.einsum(
        "blr,lw->brw", row_project, lowered, preferred_element_type=jnp.float32
    )
    root_term = lax.dot_general(
        root_project, lowered, contract_first, preferred_element_type=jnp.float32
    )
    levels = lax.axis_size("row").bit_length() - 1
    running = level_coeffs
    siblings = []
    for level_bit in range(levels):
        partner = swapped(running[level_bit:], "row", level_bit)
        siblings.append(partner[0])
        running = jnp.concatenate(
            [running[: level_bit + 1], running[level_bit + 1 :] + partner[1:]], axis=0
        )
    sibling_sum = jnp.stack(siblings, axis=0)
    root_sum = jnp.sum(lax.all_gather(lax.psum(root_term, "row"), "col", axis=0), axis=0)
    coupled = jnp.einsum(
        "blr,brw->lw",
        row_expand,
        sibling_sum.astype(jnp.bfloat16),
        preferred_element_type=jnp.float32,
    )
    root_part = jnp.dot(
        root_expand, root_sum.astype(jnp.bfloat16), preferred_element_type=jnp.float32
    )
    return dense_part + cluster_part + coupled + root_part


def solution(mesh):
    in_specs = (
        P(("row", "col"), None),
        P(("row", "col"), None),
        P(("row", "col"), None),
        P(("row", "col"), None),
        P(("row", "col"), None),
        P(None, ("row", "col"), None),
        P(None, ("row", "col"), None),
        P(("row", "col"), None),
        P(("row", "col"), None),
        P(),
    )
    out_specs = P(("row", "col"), None)
    return jax.shard_map(
        per_device, mesh=mesh, in_specs=in_specs, out_specs=out_specs, check_vma=False
    )
```

profile of v0, /device:TPU:6, one launch (start us, length us, event | category | flops | bytes accessed | tf_op | source)
XLA Modules:
  0.0 139.6 jit_solution(6744168782270515428)
XLA Ops:
  6.5 1.2 convert_element_type.16
  7.8 2.0 %convolution_bitcast_fusion.3 = f32[1,256,128]{2,1,0:T(8,128)} fusion(bf16[1024,256]{1,0:T(8,128)(2,1)} %param.19, bf16[1024,128]{1,0:T(8,128)(2,1)S(1)} %convert_element_type.16), kind=kOutput, calls=%fused_computation.11 | convolution fusion | flops 67108864 | bytes 917504 | tf_op jit(solution)/shard_map/dot_general | solution.py:47
  9.9 1.9 %sort.17 = (s32[16]{0:T(128)}, s32[16]{0:T(128)S(1)}) sort(s32[16]{0:T(128)} %param.21, s32[16]{0:T(128)S(1)} %iota.4), dimensions={0}, to_apply=%region_0.0 | sort | flops 64 | bytes 256 | tf_op jit(solution)/shard_map/jit(argsort)/sort | solution.py:33
  11.8 57.5 %all-reduce.2.cloned.1.call-done = f32[1,256,128]{2,1,0:T(8,128)} async-done(((f32[1,256,128]{2,1,0:T(8,128)}), f32[1,256,128]{2,1,0:T(8,128)}) %all-reduce.2.cloned.1.call-update) | async-done | bytes 131088 | tf_op jit(solution)/shard_map/psum | solution.py:60
  69.3 3.5 %convolution_convert_fusion.1 = bf16[2048,128]{1,0:T(8,128)(2,1)S(1)} fusion(bf16[1024,2048]{1,0:T(8,128)(2,1)} %param.14, bf16[1024,128]{1,0:T(8,128)(2,1)S(1)} %convert_element_type.16), kind=kOutput, calls=%fused_computation.3 | convolution fusion | flops 537133056 | bytes 4980736 | tf_op jit(solution)/shard_map/dot_general | solution.py:28
  72.8 0.6 gather_fusion
  73.5 0.9 broadcast_select_fusion.1
  74.4 7.0 %all-to-all-start = ((bf16[16,128,128]{2,1,0:T(8,128)(2,1)}), bf16[16,128,128]{2,1,0:T(8,128)(2,1)}, u32[]{:S(2)}, u32[]{:S(2)}) async-start(bf16[16,128,128]{2,1,0:T(8,128)(2,1)} %broadcast_select_fusion.1), calls=%async_computation | async-start | bytes 1048576 | tf_op jit(solution)/shard_map/all_to_all | solution.py:35
  81.4 2.1 %fusion.4 = f32[3,256,128]{2,1,0:T(8,128)S(1)} fusion(bf16[3,1024,256]{2,1,0:T(8,128)(2,1)} %param.17, bf16[1024,128]{1,0:T(8,128)(2,1)S(1)} %convert_element_type.16), kind=kOutput, calls=%fused_computation.15 | convolution fusion | flops 201326592 | bytes 2228224 | tf_op jit(solution)/shard_map/blr,lw->brw/dot_general | solution.py:44
  83.9 0.7 fusion.14
  84.7 0.6 collective-permute-done
  85.3 0.7 copy-done.2
  86.1 9.2 %all-to-all-done = bf16[16,128,128]{2,1,0:T(8,128)(2,1)} async-done(((bf16[16,128,128]{2,1,0:T(8,128)(2,1)}), bf16[16,128,128]{2,1,0:T(8,128)(2,1)}, u32[]{:S(2)}, u32[]{:S(2)}) %all-to-all-start) | async-done | bytes 524320 | tf_op jit(solution)/shard_map/all_to_all | solution.py:35
  95.3 6.5 %fusion = bf16[2048,128]{0,1:T(8,128)(2,1)S(1)} fusion(bf16[2048,128]{1,0:T(8,128)(2,1)} %bitcast.1, bf16[2048,2048]{1,0:T(8,128)(2,1)} %param.15), kind=kOutput, calls=%fused_computation.4 | convolution fusion | flops 1074003968 | bytes 9437184 | tf_op jit(solution)/shard_map/dot_general | solution.py:37
  101.8 1.0 copy.33
  102.8 3.6 %all-to-all-start.1 = ((bf16[16,128,128]{2,1,0:T(8,128)(2,1)}), bf16[16,128,128]{2,1,0:T(8,128)(2,1)S(1)}, u32[]{:S(2)}, u32[]{:S(2)}) async-start(bf16[16,128,128]{2,1,0:T(8,128)(2,1)} %bitcast.40), calls=%async_computation.1 | async-start | bytes 1048576 | tf_op jit(solution)/shard_map/all_to_all | solution.py:41
  106.4 0.9 slice.43
  107.3 1.6 %fusion.13 = (bf16[1,256,128]{2,1,0:T(8,128)(2,1)S(1)}, bf16[1,256,128]{2,1,0:T(8,128)(2,1)}) fusion(f32[2,256,128]{2,1,0:T(8,128)} %collective-permute-done.1, f32[2,256,128]{2,1,0:T(8,128)S(1)} %slice_add_fusion), kind=kLoop, calls=%fused_computation.33 | loop fusion | flops 65536 | bytes 458752 | tf_op jit(solution)/shard_map/slice | solution.py:55
  108.9 13.0 %all-to-all-done.1 = bf16[16,128,128]{2,1,0:T(8,128)(2,1)S(1)} async-done(((bf16[16,128,128]{2,1,0:T(8,128)(2,1)}), bf16[16,128,128]{2,1,0:T(8,128)(2,1)S(1)}, u32[]{:S(2)}, u32[]{:S(2)}) %all-to-all-start.1) | async-done | bytes 524320 | tf_op jit(solution)/shard_map/all_to_all | solution.py:41
  121.9 1.4 %gather_fusion.1 = bf16[16,128,128]{2,1,0:T(8,128)(2,1)} fusion(bf16[16,128,128]{2,1,0:T(8,128)(2,1)S(1)} %all-to-all-done.1, s32[1024]{0:T(1024)S(1)} %pad_clamp_fusion), kind=kCustom, calls=%fused_computation.1.clone | custom fusion | bytes 1048640 | tf_op jit(solution)/shard_map/jit(_take)/gather | solution.py:42
  123.3 1.2 broadcast_select_fusion
  124.5 3.5 %fusion.1 = f32[1024,128]{1,0:T(8,128)S(1)} fusion(f32[1024,128]{1,0:T(8,128)S(1)} %fusion.14, bf16[1024,2048]{1,0:T(8,128)(2,1)} %param.16, bf16[2048,128]{1,0:T(8,128)(2,1)S(1)} %bitcast.39), kind=kOutput, calls=%fused_computation.8 | convolution fusion | flops 537001984 | bytes 5767168 | tf_op jit(solution)/shard_map/dot_general | solution.py:43
  128.0 1.7 %reduce_sum.9 = bf16[256,128]{1,0:T(8,128)(2,1)S(1)} reduce(f32[16,256,128]{2,1,0:T(8,128)} %all-gather.2.cloned.1.call-done, f32[]{:T(128)} %constant.1.clone.1), dimensions={0}, to_apply=%region_2.4 | reduce | flops 491520 | bytes 2162692 | tf_op jit(solution)/shard_map/reduce_sum | solution.py:60
  130.0 2.8 %fusion.3 = f32[1024,128]{1,0:T(8,128)} fusion(f32[1024,128]{1,0:T(8,128)S(1)} %convolution_bitcast_fusion, f32[1024,128]{1,0:T(8,128)S(1)} %fusion.1, bf16[3,1024,256]{2,1,0:T(8,128)(2,1)} %param.18, bf16[1,256,128]{2,1,0:T(8,128)(2,1)} %collective-permute-done.2, bf16[1,256,128]{2,1,0:T(8,128)(2,1)S(1)} %get-tuple-element.8, ...), kind=kOutput, calls=%fused_computation.10 | convolution fusion | flops 201785344 | bytes 3342336 | tf_op jit(solution)/shard_map/blr,brw->lw/dot_general | solution.py:61
  (26 shorter events, 0.9 us)
Async XLA Ops:
  6.5 77.4 %copy-start = (bf16[1024,1024]{1,0:T(8,128)(2,1)S(1)}, bf16[1024,1024]{1,0:T(8,128)(2,1)}, u32[]{:S(2)}) copy-start(bf16[1024,1024]{1,0:T(8,128)(2,1)} %param.13) | copy-start | bytes 6291460
  6.5 62.7 %all-reduce.2.cloned.1.call-start = ((), (), s32[]{:S(2)}) async-start(), calls=%async_computation.2 | async-start | bytes 262144 | tf_op jit(solution)/shard_map/psum | solution.py:60
  9.8 118.1 %all-gather.2.cloned.1.call-start = ((), (), s32[]{:S(2)}) async-start(), calls=%async_computation.3 | async-start | bytes 2228224 | tf_op jit(solution)/shard_map/all_gather | solution.py:60
  74.4 20.9 %all-to-all-start = ((bf16[16,128,128]{2,1,0:T(8,128)(2,1)}), bf16[16,128,128]{2,1,0:T(8,128)(2,1)}, u32[]{:S(2)}, u32[]{:S(2)}) async-start(bf16[16,128,128]{2,1,0:T(8,128)(2,1)} %broadcast_select_fusion.1), calls=%async_computation | async-start | bytes 1048576 | tf_op jit(solution)/shard_map/all_to_all | solution.py:35
  81.4 3.2 %copy-start.3 = (s32[16]{0:T(128)S(1)}, s32[16]{0:T(128)}, u32[]{:S(2)}) copy-start(s32[16]{0:T(128)} %param.21) | copy-start | bytes 196
  83.5 1.8 %collective-permute-start = (f32[3,256,128]{2,1,0:T(8,128)S(1)}, f32[3,256,128]{2,1,0:T(8,128)S(1)}, u32[]{:S(2)}, u32[]{:S(2)}) collective-permute-start(f32[3,256,128]{2,1,0:T(8,128)S(1)} %fusion.4), channel_id=1, source_target_pairs={{0,16},{16,0},{32,48},{48,32},{64,80},{80,64},{96,112},{112,96},{1... | collective-permute-start | bytes 1179656 | tf_op jit(solution)/shard_map/ppermute | solution.py:10
  85.3 0.8 copy-start.2
  86.0 21.2 %collective-permute-start.1 = (f32[2,256,128]{2,1,0:T(8,128)S(1)}, f32[2,256,128]{2,1,0:T(8,128)}, u32[]{:S(2)}, u32[]{:S(2)}) collective-permute-start(f32[2,256,128]{2,1,0:T(8,128)S(1)} %slice_add_fusion), channel_id=1, source_target_pairs={{0,32},{16,48},{32,0},{48,16},{64,96},{80,112},{96,64},{112,80},{1... | collective-permute-start | bytes 786440 | tf_op jit(solution)/shard_map/ppermute | solution.py:10
  102.8 19.1 %all-to-all-start.1 = ((bf16[16,128,128]{2,1,0:T(8,128)(2,1)}), bf16[16,128,128]{2,1,0:T(8,128)(2,1)S(1)}, u32[]{:S(2)}, u32[]{:S(2)}) async-start(bf16[16,128,128]{2,1,0:T(8,128)(2,1)} %bitcast.40), calls=%async_computation.1 | async-start | bytes 1048576 | tf_op jit(solution)/shard_map/all_to_all | solution.py:41
  108.9 21.1 %collective-permute-start.2 = (bf16[1,256,128]{2,1,0:T(8,128)(2,1)}, bf16[1,256,128]{2,1,0:T(8,128)(2,1)}, u32[]{:S(2)}, u32[]{:S(2)}) collective-permute-start(bf16[1,256,128]{2,1,0:T(8,128)(2,1)} %get-tuple-element.9), channel_id=1, source_target_pairs={{0,64},{16,80},{32,96},{48,112},{64,0},{80,16},{96,32},{112,48},{1... | collective-permute-start | bytes 196616 | tf_op jit(solution)/shard_map/ppermute | solution.py:10
  127.9 1.8 %copy-start.1 = (bf16[1024,256]{1,0:T(8,128)(2,1)S(1)}, bf16[1024,256]{1,0:T(8,128)(2,1)}, u32[]{:S(2)}) copy-start(bf16[1024,256]{1,0:T(8,128)(2,1)} %param.20) | copy-start | bytes 1572868
Sparse Core Ops, SparseCore 0:
  9.9 59.2 all-reduce.1
  71.6 53.5 all-gather.1
where the time goes:
time: 140 us
  waiting for transfers between devices  80.3 us (57%)
  matrix products  21.3 us (15%)
  between operations  13.6 us (10%)
  starting transfers between devices  11.1 us (8%)
  other arithmetic  8.62 us (6%)
  local copies, waits for them, and re-layouts  4.72 us (3%)
    psum x1, waiting for transfers between devices, per_device(): lax.psum(root_term, 'row')  57.5 us
    all_to_all x1, waiting for transfers between devices, per_device(): lax.all_to_all(mixed_rows, 'col', split_axis=0, concat_axis=0, tiled=True)  13 us
    all_to_all x1, waiting for transfers between devices, per_device(): lax.all_to_all(outgoing, 'col', split_axis=0, concat_axis=0, tiled=True)  9.2 us
    all_to_all x1, starting transfers between devices, per_device(): lax.all_to_all(outgoing, 'col', split_axis=0, concat_axis=0, tiled=True)  7.03 us
    dot_general x1, matrix products, per_device(): jnp.dot(middle, arrived.reshape(-1, shape_now[2]), preferred_element_type...  6.49 us
    all_to_all x1, starting transfers between devices, per_device(): lax.all_to_all(mixed_rows, 'col', split_axis=0, concat_axis=0, tiled=True)  3.57 us
    dot_general x1, matrix products, per_device(): lax.dot_general(compress, lowered, contract_first, preferred_element_type...  3.5 us
    dot_general x1, matrix products, per_device(): cluster_part = jnp.dot(expand, ordered, preferred_element_type=jnp.float32)  3.45 us
  transfers between devices with their start and end apart: 7, of which 4 were waited for; matrix products, arithmetic and copies ran while one was open for 20% of the time, Pallas kernels for 0%

commit v1 on v0

--- a/solution.py
+++ b/solution.py
@@ -57,7 +57,9 @@
             [running[: level_bit + 1], running[level_bit + 1 :] + partner[1:]], axis=0
         )
     sibling_sum = jnp.stack(siblings, axis=0)
-    root_sum = jnp.sum(lax.all_gather(lax.psum(root_term, "row"), "col", axis=0), axis=0)
+    root_sum = jnp.sum(
+        lax.all_gather(jnp.sum(lax.all_gather(root_term, "row"), axis=0), "col", axis=0), axis=0
+    )
     coupled = jnp.einsum(
         "blr,brw->lw",
         row_expand,

time: 140 us -> 108 us (0.77); the launches traced: 140 us -> 106 us
  waiting for transfers between devices: 80.3 us -> 42.4 us
  starting transfers between devices: 11.1 us -> 13.3 us
  other arithmetic: 8.62 us -> 10.6 us
    psum x1 -> x0, waiting for transfers between devices: 57.5 us -> none  [per_device(): lax.psum(root_term, 'row')]
    all_gather x1 -> x2, waiting for transfers between devices: 0.02 us -> 22.1 us  [the longest x1 22.1 us: per_device(): lax.all_gather(root_term, 'row')]
    ppermute x3, starting transfers between devices: 0.45 us -> 2.68 us  [swapped(): lax.ppermute(x, axis, [(i, i ^ 1 << bit) for i in range(lax.axis_size(axi...]
    reduce_sum x1 -> x2, other arithmetic: 1.75 us -> 3.69 us  [the longest x1 1.94 us: per_device(): jnp.sum(lax.all_gather(root_term, 'row'), axis=0)]
    all_to_all x1, waiting for transfers between devices: 13 us -> 11.5 us  [per_device(): lax.all_to_all(mixed_rows, 'col', split_axis=0, concat_axis=0, tiled=True)]
  transfers between devices with their start and end apart: 7 -> 7, of which waited for: 4 -> 4; matrix products, arithmetic and copies ran while one was open for 20% -> 26% of each run, Pallas kernels for 0% -> 0%
where the time goes in v1:
time: 108 us; the launch traced here: 106 us
  waiting for transfers between devices  42.4 us (39%)
  matrix products  21.3 us (20%)
  between operations  13.6 us (13%)
  starting transfers between devices  13.3 us (12%)
  other arithmetic  10.6 us (10%)
  local copies, waits for them, and re-layouts  4.72 us (4%)
    all_gather x1, waiting for transfers between devices, per_device(): lax.all_gather(root_term, 'row')  22.1 us
    all_to_all x1, waiting for transfers between devices, per_device(): lax.all_to_all(mixed_rows, 'col', split_axis=0, concat_axis=0, tiled=True)  11.5 us
    all_to_all x1, waiting for transfers between devices, per_device(): lax.all_to_all(outgoing, 'col', split_axis=0, concat_axis=0, tiled=True)  7.84 us
    all_to_all x1, starting transfers between devices, per_device(): lax.all_to_all(outgoing, 'col', split_axis=0, concat_axis=0, tiled=True)  7.03 us
    dot_general x1, matrix products, per_device(): jnp.dot(middle, arrived.reshape(-1, shape_now[2]), preferred_element_type...  6.48 us
    all_to_all x1, starting transfers between devices, per_device(): lax.all_to_all(mixed_rows, 'col', split_axis=0, concat_axis=0, tiled=True)  3.59 us
    dot_general x1, matrix products, per_device(): lax.dot_general(compress, lowered, contract_first, preferred_element_type...  3.5 us
    dot_general x1, matrix products, per_device(): cluster_part = jnp.dot(expand, ordered, preferred_element_type=jnp.float32)  3.45 us
  transfers between devices with their start and end apart: 7, of which 4 were waited for; matrix products, arithmetic and copies ran while one was open for 26% of the time, Pallas kernels for 0%

profile of v1, /device:TPU:6, one launch (start us, length us, event | category | flops | bytes accessed | tf_op | source)
XLA Modules:
  0.0 106.0 jit_solution(2589416082276399458)
XLA Ops:
  6.5 1.2 %convert_element_type.16 = bf16[1024,128]{1,0:T(8,128)(2,1)S(1)} convert(f32[1024,128]{1,0:T(8,128)} %param.12) | non-fusion elementwise | flops 131072 | bytes 786432 | tf_op jit(solution)/shard_map/convert_element_type | solution.py:25
  7.8 2.0 %fusion.15 = f32[256,128]{1,0:T(8,128)} fusion(bf16[1024,256]{1,0:T(8,128)(2,1)} %param.19, bf16[1024,128]{1,0:T(8,128)(2,1)S(1)} %convert_element_type.16), kind=kOutput, calls=%fused_computation.34 | convolution fusion | flops 67108864 | bytes 917504 | tf_op jit(solution)/shard_map/dot_general | solution.py:47
  9.9 2.0 %sort.17 = (s32[16]{0:T(128)}, s32[16]{0:T(128)S(1)}) sort(s32[16]{0:T(128)} %param.21, s32[16]{0:T(128)S(1)} %iota.4), dimensions={0}, to_apply=%region_0.0 | sort | flops 64 | bytes 256 | tf_op jit(solution)/shard_map/jit(argsort)/sort | solution.py:33
  11.8 22.1 %all-gather.5.cloned.1.call-done = f32[2048,128]{1,0:T(8,128)} async-done(((f32[256,128]{1,0:T(8,128)}), f32[2048,128]{1,0:T(8,128)}) %all-gather.5.cloned.1.call-update) | async-done | bytes 1048592 | tf_op jit(solution)/shard_map/all_gather | solution.py:61
  34.0 1.9 %reduce_sum.18 = f32[256,128]{1,0:T(8,128)} reduce(f32[8,256,128]{2,1,0:T(8,128)} %bitcast.42, f32[]{:T(128)} %constant.1.clone.1), dimensions={0}, to_apply=%region_1.3 | reduce | flops 229376 | bytes 1179652 | tf_op jit(solution)/shard_map/reduce_sum | solution.py:61
  36.0 3.5 %convolution_convert_fusion.1 = bf16[2048,128]{1,0:T(8,128)(2,1)S(1)} fusion(bf16[1024,2048]{1,0:T(8,128)(2,1)} %param.14, bf16[1024,128]{1,0:T(8,128)(2,1)S(1)} %convert_element_type.16), kind=kOutput, calls=%fused_computation.3 | convolution fusion | flops 537133056 | bytes 4980736 | tf_op jit(solution)/shard_map/dot_general | solution.py:28
  40.1 0.9 broadcast_select_fusion.1
  41.0 7.0 %all-to-all-start = ((bf16[16,128,128]{2,1,0:T(8,128)(2,1)}), bf16[16,128,128]{2,1,0:T(8,128)(2,1)}, u32[]{:S(2)}, u32[]{:S(2)}) async-start(bf16[16,128,128]{2,1,0:T(8,128)(2,1)} %broadcast_select_fusion.1), calls=%async_computation | async-start | bytes 1048576 | tf_op jit(solution)/shard_map/all_to_all | solution.py:35
  48.1 2.0 %fusion.4 = f32[3,256,128]{2,1,0:T(8,128)S(1)} fusion(bf16[3,1024,256]{2,1,0:T(8,128)(2,1)} %param.17, bf16[1024,128]{1,0:T(8,128)(2,1)S(1)} %convert_element_type.16), kind=kOutput, calls=%fused_computation.14 | convolution fusion | flops 201326592 | bytes 2228224 | tf_op jit(solution)/shard_map/blr,lw->brw/dot_general | solution.py:44
  51.0 1.0 collective-permute-done
  52.7 1.1 %collective-permute-start.1 = (f32[2,256,128]{2,1,0:T(8,128)S(1)}, f32[2,256,128]{2,1,0:T(8,128)}, u32[]{:S(2)}, u32[]{:S(2)}) collective-permute-start(f32[2,256,128]{2,1,0:T(8,128)S(1)} %slice_add_fusion), channel_id=1, source_target_pairs={{0,32},{16,48},{32,0},{48,16},{64,96},{80,112},{96,64},{112,80},{1... | collective-permute-start | bytes 786440 | tf_op jit(solution)/shard_map/ppermute | solution.py:10
  53.8 7.8 %all-to-all-done = bf16[16,128,128]{2,1,0:T(8,128)(2,1)} async-done(((bf16[16,128,128]{2,1,0:T(8,128)(2,1)}), bf16[16,128,128]{2,1,0:T(8,128)(2,1)}, u32[]{:S(2)}, u32[]{:S(2)}) %all-to-all-start) | async-done | bytes 524320 | tf_op jit(solution)/shard_map/all_to_all | solution.py:35
  61.7 6.5 %fusion = bf16[2048,128]{0,1:T(8,128)(2,1)S(1)} fusion(bf16[2048,128]{1,0:T(8,128)(2,1)} %bitcast.1, bf16[2048,2048]{1,0:T(8,128)(2,1)} %param.15), kind=kOutput, calls=%fused_computation.4 | convolution fusion | flops 1074003968 | bytes 9437184 | tf_op jit(solution)/shard_map/dot_general | solution.py:37
  68.1 1.0 copy.33
  69.1 3.6 %all-to-all-start.1 = ((bf16[16,128,128]{2,1,0:T(8,128)(2,1)}), bf16[16,128,128]{2,1,0:T(8,128)(2,1)S(1)}, u32[]{:S(2)}, u32[]{:S(2)}) async-start(bf16[16,128,128]{2,1,0:T(8,128)(2,1)} %bitcast.41), calls=%async_computation.1 | async-start | bytes 1048576 | tf_op jit(solution)/shard_map/all_to_all | solution.py:41
  72.8 0.9 slice.43
  73.7 1.6 %fusion.13 = (bf16[1,256,128]{2,1,0:T(8,128)(2,1)S(1)}, bf16[1,256,128]{2,1,0:T(8,128)(2,1)}) fusion(f32[2,256,128]{2,1,0:T(8,128)} %collective-permute-done.1, f32[2,256,128]{2,1,0:T(8,128)S(1)} %slice_add_fusion), kind=kLoop, calls=%fused_computation.32 | loop fusion | flops 65536 | bytes 458752 | tf_op jit(solution)/shard_map/slice | solution.py:55
  75.3 1.5 %collective-permute-start.2 = (bf16[1,256,128]{2,1,0:T(8,128)(2,1)}, bf16[1,256,128]{2,1,0:T(8,128)(2,1)}, u32[]{:S(2)}, u32[]{:S(2)}) collective-permute-start(bf16[1,256,128]{2,1,0:T(8,128)(2,1)} %get-tuple-element.9), channel_id=1, source_target_pairs={{0,64},{16,80},{32,96},{48,112},{64,0},{80,16},{96,32},{112,48},{1... | collective-permute-start | bytes 196616 | tf_op jit(solution)/shard_map/ppermute | solution.py:10
  76.8 11.5 %all-to-all-done.1 = bf16[16,128,128]{2,1,0:T(8,128)(2,1)S(1)} async-done(((bf16[16,128,128]{2,1,0:T(8,128)(2,1)}), bf16[16,128,128]{2,1,0:T(8,128)(2,1)S(1)}, u32[]{:S(2)}, u32[]{:S(2)}) %all-to-all-start.1) | async-done | bytes 524320 | tf_op jit(solution)/shard_map/all_to_all | solution.py:41
  88.2 1.4 %gather_fusion.1 = bf16[16,128,128]{2,1,0:T(8,128)(2,1)} fusion(bf16[16,128,128]{2,1,0:T(8,128)(2,1)S(1)} %all-to-all-done.1, s32[1024]{0:T(1024)S(1)} %pad_clamp_fusion), kind=kCustom, calls=%fused_computation.1.clone | custom fusion | bytes 1048640 | tf_op jit(solution)/shard_map/jit(_take)/gather | solution.py:42
  89.6 1.2 %broadcast_select_fusion = bf16[16,128,128]{2,1,0:T(8,128)(2,1)S(1)} fusion(bf16[16,128,128]{2,1,0:T(8,128)(2,1)} %gather_fusion.1, pred[16]{0:T(512)(128)(4,1)S(1)} %compare_and_fusion), kind=kLoop, calls=%fused_computation.11 | loop fusion | flops 262144 | bytes 1048592 | tf_op jit(solution)/shard_map/jit(_take)/select_n | solution.py:42
  90.8 3.5 %fusion.1 = f32[1024,128]{1,0:T(8,128)S(1)} fusion(f32[1024,128]{1,0:T(8,128)S(1)} %fusion.14, bf16[1024,2048]{1,0:T(8,128)(2,1)} %param.16, bf16[2048,128]{1,0:T(8,128)(2,1)S(1)} %bitcast.40), kind=kOutput, calls=%fused_computation.8 | convolution fusion | flops 537001984 | bytes 5767168 | tf_op jit(solution)/shard_map/dot_general | solution.py:43
  94.3 1.7 %reduce_sum.19 = bf16[256,128]{1,0:T(8,128)(2,1)S(1)} reduce(f32[16,256,128]{2,1,0:T(8,128)} %bitcast.39, f32[]{:T(128)} %constant.1.clone.1), dimensions={0}, to_apply=%region_2.4 | reduce | flops 491520 | bytes 2162692 | tf_op jit(solution)/shard_map/reduce_sum | solution.py:60
  96.4 2.8 %fusion.3 = f32[1024,128]{1,0:T(8,128)} fusion(f32[1024,128]{1,0:T(8,128)S(1)} %convolution_bitcast_fusion, f32[1024,128]{1,0:T(8,128)S(1)} %fusion.1, bf16[3,1024,256]{2,1,0:T(8,128)(2,1)} %param.18, bf16[1,256,128]{2,1,0:T(8,128)(2,1)} %collective-permute-done.2, bf16[1,256,128]{2,1,0:T(8,128)(2,1)S(1)} %get-tuple-element.8, ...), kind=kOutput, calls=%fused_computation.10 | convolution fusion | flops 201785344 | bytes 3342336 | tf_op jit(solution)/shard_map/blr,brw->lw/dot_general | solution.py:63
  (27 shorter events, 2.6 us)
Async XLA Ops:
  6.5 43.7 %copy-start = (bf16[1024,1024]{1,0:T(8,128)(2,1)S(1)}, bf16[1024,1024]{1,0:T(8,128)(2,1)}, u32[]{:S(2)}) copy-start(bf16[1024,1024]{1,0:T(8,128)(2,1)} %param.13) | copy-start | bytes 6291460
  6.5 27.4 %all-gather.5.cloned.1.call-start = ((), (), s32[]{:S(2)}) async-start(), calls=%async_computation.2 | async-start | bytes 1179648 | tf_op jit(solution)/shard_map/all_gather | solution.py:61
  9.8 84.5 %all-gather.7.cloned.1.call-start = ((), (), s32[]{:S(2)}) async-start(), calls=%async_computation.3 | async-start | bytes 2228224 | tf_op jit(solution)/shard_map/all_gather | solution.py:61
  41.0 20.6 %all-to-all-start = ((bf16[16,128,128]{2,1,0:T(8,128)(2,1)}), bf16[16,128,128]{2,1,0:T(8,128)(2,1)}, u32[]{:S(2)}, u32[]{:S(2)}) async-start(bf16[16,128,128]{2,1,0:T(8,128)(2,1)} %broadcast_select_fusion.1), calls=%async_computation | async-start | bytes 1048576 | tf_op jit(solution)/shard_map/all_to_all | solution.py:35
  48.1 2.9 %copy-start.3 = (s32[16]{0:T(128)S(1)}, s32[16]{0:T(128)}, u32[]{:S(2)}) copy-start(s32[16]{0:T(128)} %param.21) | copy-start | bytes 196
  50.1 1.8 %collective-permute-start = (f32[3,256,128]{2,1,0:T(8,128)S(1)}, f32[3,256,128]{2,1,0:T(8,128)S(1)}, u32[]{:S(2)}, u32[]{:S(2)}) collective-permute-start(f32[3,256,128]{2,1,0:T(8,128)S(1)} %fusion.4), channel_id=1, source_target_pairs={{0,16},{16,0},{32,48},{48,32},{64,80},{80,64},{96,112},{112,96},{1... | collective-permute-start | bytes 1179656 | tf_op jit(solution)/shard_map/ppermute | solution.py:10
  51.9 0.8 copy-start.2
  52.7 21.0 %collective-permute-start.1 = (f32[2,256,128]{2,1,0:T(8,128)S(1)}, f32[2,256,128]{2,1,0:T(8,128)}, u32[]{:S(2)}, u32[]{:S(2)}) collective-permute-start(f32[2,256,128]{2,1,0:T(8,128)S(1)} %slice_add_fusion), channel_id=1, source_target_pairs={{0,32},{16,48},{32,0},{48,16},{64,96},{80,112},{96,64},{112,80},{1... | collective-permute-start | bytes 786440 | tf_op jit(solution)/shard_map/ppermute | solution.py:10
  69.1 19.1 %all-to-all-start.1 = ((bf16[16,128,128]{2,1,0:T(8,128)(2,1)}), bf16[16,128,128]{2,1,0:T(8,128)(2,1)S(1)}, u32[]{:S(2)}, u32[]{:S(2)}) async-start(bf16[16,128,128]{2,1,0:T(8,128)(2,1)} %bitcast.41), calls=%async_computation.1 | async-start | bytes 1048576 | tf_op jit(solution)/shard_map/all_to_all | solution.py:41
  75.3 21.0 %collective-permute-start.2 = (bf16[1,256,128]{2,1,0:T(8,128)(2,1)}, bf16[1,256,128]{2,1,0:T(8,128)(2,1)}, u32[]{:S(2)}, u32[]{:S(2)}) collective-permute-start(bf16[1,256,128]{2,1,0:T(8,128)(2,1)} %get-tuple-element.9), channel_id=1, source_target_pairs={{0,64},{16,80},{32,96},{48,112},{64,0},{80,16},{96,32},{112,48},{1... | collective-permute-start | bytes 196616 | tf_op jit(solution)/shard_map/ppermute | solution.py:10
  94.3 1.8 %copy-start.1 = (bf16[1024,256]{1,0:T(8,128)(2,1)S(1)}, bf16[1024,256]{1,0:T(8,128)(2,1)}, u32[]{:S(2)}) copy-start(bf16[1024,256]{1,0:T(8,128)(2,1)} %param.20) | copy-start | bytes 1572868
Sparse Core Ops, SparseCore 0:
  9.9 23.9 all-gather.4
  36.1 55.1 all-gather.6
